TPU v7x, 512 devices: a whole 4x8x8 slice. The times are simulated.
512 devices in a mesh: row: 16 (over y, core), col: 32 (over x, z).
Axes of the slice: x: 4, y: 8, z: 8, core: 2. Of those that a mesh axis runs over, the one named last changes fastest.
Arguments:
- excitons: float32 [1024, 1024], P('row', 'col'), may hold values from -500 to 500
- valence_energy: float32 [1024], P('row'), may hold values from -3 to -1
- conduction_energy: float32 [1024], P('col'), may hold values from 1 to 3
- psi_valence: float32 [4096, 1024], P('row', 'col'), may hold values from -0.1875 to 0.1875
- psi_conduction: float32 [4096, 1024], P('col', 'row'), may hold values from -0.1875 to 0.1875
- screened: float32 [4096, 4096], P('row', 'col'), may hold values from -0.9 to 0.975, as said below
Outputs:
- next_vector: float32 [1024, 1024], P('row', 'col')
- coefficients: float32 [4], replicated
Inputs may be any that keep to these rules, and one draw needn't show every extreme that they name: symmetric: screened[p, p'] = screened[p', p].
All inputs are finite; a program needn't handle non-finite values.
Results may differ from a plain program's by a relative error of at most 0.0003.
Values sent between devices are 32-bit elements; how exact they have to be, the bound alone decides.
No kernel may reach another device: no remote copies, remote signals or barrier semaphores. Data moves between devices by JAX's collectives and lax.ppermute only.
A program may use at most 64 MiB of HBM per device.

v0:
```python
import functools
import jax
import jax.numpy as jnp
from jax import lax
from jax.sharding import Mesh
from jax.sharding import PartitionSpec as P

NV = 1024
NC = 1024
STEPS = 2
COL = ("col_0", "col_1")
ROW = ("row_0", "row_1")
ROW_COL = ("row_0", "row_1", "col_0", "col_1")
EPS = 1e-06


def copy_for_each(value, axis):
    size = lax.axis_size(axis)
    return lax.all_to_all(
        jnp.broadcast_to(value[None], (size, *value.shape)), axis, 0, 0, tiled=True
    )


def in_order(parts, dim):
    parts = jnp.moveaxis(parts, 0, dim)
    dims = parts.shape
    return parts.reshape(*dims[:dim], dims[dim] * dims[dim + 1], *dims[dim + 2 :])


def gathered_copies(value, axis, dim):
    parts = copy_for_each(value, axis)
    return in_order(parts, dim)


def cut_along(value, dim, size):
    dims = value.shape
    parts = value.reshape(*dims[:dim], size, dims[dim] // size, *dims[dim + 1 :])
    return jnp.moveaxis(parts, dim, 0)


def sum_at_owner(value, axis, dim):
    parts = cut_along(value, dim, lax.axis_size(axis))
    arrived = lax.all_to_all(parts, axis, split_axis=0, concat_axis=0, tiled=True)
    return arrived.sum(axis=0)


def over_axes(value, axes):
    return functools.reduce(lax.psum, axes, value)


def shards(excitons, valence_energy, conduction_energy, psi_valence, psi_conduction, screened):
    high = lax.Precision.HIGHEST
    count = NV * NC
    energy_gap = conduction_energy[None, :] - valence_energy[:, None]
    total = over_axes(jnp.sum(excitons * excitons), ROW_COL)
    vector = excitons / jnp.sqrt(total / count + EPS)
    previous = jnp.zeros_like(vector)
    beta_prev = jnp.zeros((), jnp.float32)
    values = []
    for step in range(STEPS):
        panel_valence = gathered_copies(psi_valence, COL, 1)
        panel_conduction = gathered_copies(psi_conduction, ROW, 1)
        full_rows = gathered_copies(vector, COL, 1)
        image_block = jnp.dot(full_rows, panel_conduction.T, precision=high)
        image_columns = lax.all_gather(image_block, ROW, axis=0, tiled=True)
        points = jnp.dot(panel_valence, image_columns, precision=high)
        weighted = points * screened
        back_valence = sum_at_owner(jnp.dot(panel_valence.T, weighted, precision=high), ROW, 0)
        back_flipped = back_valence.T
        kernel_flipped = sum_at_owner(
            jnp.dot(panel_conduction.T, back_flipped, precision=high), COL, 0
        )
        image = energy_gap * vector - kernel_flipped.T
        cross, square, older = (
            over_axes(jnp.sum(vector * image), ROW_COL),
            over_axes(jnp.sum(image * image), ROW_COL),
            over_axes(jnp.sum(previous * image), ROW_COL),
        )
        alpha = cross / count
        residual = image - alpha * vector - beta_prev * previous
        squared = (
            square / count - alpha * alpha - 2.0 * beta_prev * older / count + beta_prev * beta_prev
        )
        beta = jnp.sqrt(squared + EPS)
        previous = vector
        vector = residual / beta
        beta_prev = beta
        values.append(alpha)
        values.append(beta)
    return (vector, jnp.stack(values))


def solution(mesh):
    finer = Mesh(mesh.devices.reshape(8, 2, 4, 8), ("row_0", "row_1", "col_0", "col_1"))
    placed = (P(ROW, COL), P(ROW), P(COL), P(ROW, COL), P(COL, ROW), P(ROW, COL))
    return jax.shard_map(
        shards, mesh=finer, in_specs=placed, out_specs=(P(ROW, COL), P()), check_vma=False
    )
```

profile of v0, /device:TPU:8, one launch (start us, length us, event | category | flops | bytes accessed | tf_op | source)
XLA Modules:
  0.0 351.9 jit_solution(16004232356385606627)
XLA Ops:
  0.6 1.4 multiply_reduce_fusion.6
  2.0 20.6 %psum.196 = f32[]{:T(128)} all-reduce(f32[]{:T(128)} %multiply_reduce_fusion.6), channel_id=1, replica_groups=mesh['row_0'=8,'row_1'=2,'col_0'=4,'col_1'=8] {'row_0'}, use_global_device_ids=true, to_apply=%region_1.0 | all-reduce | flops 1 | bytes 8 | tf_op jit(solution)/shard_map/psum | solution.py:48
  22.6 3.1 psum.197
  25.7 8.3 %psum.198 = f32[]{:T(128)} all-reduce(f32[]{:T(128)} %psum.197), channel_id=1, replica_groups=mesh['row_0'=8,'row_1'=2,'col_0'=4,'col_1'=8] {'col_0'}, use_global_device_ids=true, to_apply=%region_3.0 | all-reduce | flops 1 | bytes 8 | tf_op jit(solution)/shard_map/psum | solution.py:48
  34.0 22.8 %psum.199 = f32[]{:T(128)} all-reduce(f32[]{:T(128)} %psum.198), channel_id=1, replica_groups=mesh['row_0'=8,'row_1'=2,'col_0'=4,'col_1'=8] {'col_1'}, use_global_device_ids=true, to_apply=%region_4.0 | all-reduce | flops 1 | bytes 8 | tf_op jit(solution)/shard_map/psum | solution.py:48
  57.5 0.1 broadcast_bitcast_fusion.1
  57.6 0.3 reshape.44
  57.9 0.0 copy-start.2
  57.9 14.0 %all_to_all.42 = f32[32,1,2048]{2,1,0:T(1,128)S(1)} all-to-all(f32[32,1,2048]{2,1,0:T(1,128)S(1)} %reshape.44), channel_id=1, replica_groups=mesh['row_0'=8,'row_1'=2,'col_0'=4,'col_1'=8] {'col_0','col_1'}, dimensions={0} | all-to-all | bytes 524288 | tf_op jit(solution)/shard_map/all_to_all | solution.py:19
  72.0 20.4 %all_to_all.43 = f32[16,128,64]{1,2,0:T(8,128)S(1)} all-to-all(f32[16,128,64]{1,2,0:T(8,128)S(1)} %broadcast_in_dim.11), channel_id=1, replica_groups=mesh['row_0'=8,'row_1'=2,'col_0'=4,'col_1'=8] {'row_0','row_1'}, dimensions={0} | all-to-all | bytes 1048576 | tf_op jit(solution)/shard_map/all_to_all | solution.py:19
  92.4 1.1 broadcast_in_dim.12
  93.5 4.7 %all-to-all-start.2 = ((f32[32,256,32]{1,2,0:T(8,128)}), f32[32,256,32]{1,2,0:T(8,128)S(1)}, u32[]{:S(2)}, u32[]{:S(2)}) async-start(f32[32,256,32]{1,2,0:T(8,128)} %broadcast_in_dim.12), calls=%async_computation.2 | async-start | bytes 2097152 | tf_op jit(solution)/shard_map/all_to_all | solution.py:19
  98.1 0.5 broadcast.6
  98.6 1.3 reduce
  99.9 0.2 reshape.45
  100.1 1.0 fusion.4
  101.2 0.0 copy-start.1
  101.2 17.7 %all_gather.6 = f32[1024,128]{1,0:T(8,128)S(1)} all-gather(f32[64,128]{1,0:T(8,128)S(1)} %fusion.4), channel_id=1, replica_groups=mesh['row_0'=8,'row_1'=2,'col_0'=4,'col_1'=8] {'row_0','row_1'}, dimensions={0}, use_global_device_ids=true | all-gather | bytes 557056 | tf_op jit(solution)/shard_map/all_gather | solution.py:65
  118.9 8.2 %all-to-all-done.2 = f32[32,256,32]{1,2,0:T(8,128)S(1)} async-done(((f32[32,256,32]{1,2,0:T(8,128)}), f32[32,256,32]{1,2,0:T(8,128)S(1)}, u32[]{:S(2)}, u32[]{:S(2)}) %all-to-all-start.2) | async-done | bytes 1048608 | tf_op jit(solution)/shard_map/all_to_all | solution.py:19
  127.0 1.8 fusion.1
  128.8 1.2 convolution_bitcast_fusion.1
  130.1 0.2 copy.12
  130.3 20.0 %all_to_all.44 = f32[16,64,128]{2,1,0:T(8,128)S(1)} all-to-all(f32[16,64,128]{2,1,0:T(8,128)S(1)} %bitcast.89), channel_id=1, replica_groups=mesh['row_0'=8,'row_1'=2,'col_0'=4,'col_1'=8] {'row_0','row_1'}, dimensions={0} | all-to-all | bytes 1048576 | tf_op jit(solution)/shard_map/all_to_all | solution.py:43
  150.3 0.7 convolution_bitcast_fusion.3
  151.0 0.2 copy.13
  151.2 0.3 reshape.46
  151.5 17.6 %all_to_all.45 = f32[32,1,2048]{2,1,0:T(1,128)S(1)} all-to-all(f32[32,1,2048]{2,1,0:T(1,128)S(1)} %reshape.46), channel_id=1, replica_groups=mesh['row_0'=8,'row_1'=2,'col_0'=4,'col_1'=8] {'col_0','col_1'}, dimensions={0} | all-to-all | bytes 524288 | tf_op jit(solution)/shard_map/all_to_all | solution.py:43
  169.2 1.3 reduce.1
  170.4 0.2 reshape.47
  170.7 0.1 reduce_sum.101
  170.7 0.6 copy-done.4
  171.3 0.0 copy-done.5
  171.3 0.7 multiply_reduce_fusion.3
  172.1 15.7 %all-reduce.3 = (f32[]{:T(128)}, f32[]{:T(128)}, f32[]{:T(128)}) all-reduce(f32[]{:T(128)} %get-tuple-element.6, f32[]{:T(128)} %get-tuple-element.7, f32[]{:T(128)} %get-tuple-element.5), channel_id=1, replica_groups=mesh['row_0'=8,'row_1'=2,'col_0'=4,'col_1'=8] {'row_0'}, use_global_device_ids=true, to_apply=%region_13.0 | all-reduce | flops 3 | bytes 24 | tf_op jit(solution)/shard_map/psum | solution.py:48
  187.8 3.1 all-reduce.7
  190.9 10.2 %all-reduce.5 = (f32[]{:T(128)}, f32[]{:T(128)}, f32[]{:T(128)}) all-reduce(f32[]{:T(128)} %get-tuple-element.29, f32[]{:T(128)} %get-tuple-element.30, f32[]{:T(128)} %get-tuple-element.31), channel_id=1, replica_groups=mesh['row_0'=8,'row_1'=2,'col_0'=4,'col_1'=8] {'col_0'}, use_global_device_ids=true, to_apply=%region_15.0 | all-reduce | flops 3 | bytes 24 | tf_op jit(solution)/shard_map/psum | solution.py:48
  201.1 17.3 %all-reduce.1 = (f32[]{:T(128)}, f32[]{:T(128)}, f32[]{:T(128)}) all-reduce(f32[]{:T(128)} %get-tuple-element.23, f32[]{:T(128)} %get-tuple-element.24, f32[]{:T(128)} %get-tuple-element.25), channel_id=1, replica_groups=mesh['row_0'=8,'row_1'=2,'col_0'=4,'col_1'=8] {'col_1'}, use_global_device_ids=true, to_apply=%region_16.0 | all-reduce | flops 3 | bytes 24 | tf_op jit(solution)/shard_map/psum | solution.py:48
  221.7 0.1 subtract_divide_fusion.1
  221.8 0.1 broadcast_bitcast_fusion
  221.8 0.3 reshape.48
  222.2 15.4 %all_to_all.46 = f32[32,1,2048]{2,1,0:T(1,128)S(1)} all-to-all(f32[32,1,2048]{2,1,0:T(1,128)S(1)} %reshape.48), channel_id=1, replica_groups=mesh['row_0'=8,'row_1'=2,'col_0'=4,'col_1'=8] {'col_0','col_1'}, dimensions={0} | all-to-all | bytes 524288 | tf_op jit(solution)/shard_map/all_to_all | solution.py:19
  237.5 1.3 reduce.2
  238.8 0.2 reshape.49
  239.0 1.0 fusion.5
  240.0 15.7 %all_gather.7 = f32[1024,128]{1,0:T(8,128)S(1)} all-gather(f32[64,128]{1,0:T(8,128)S(1)} %fusion.5), channel_id=1, replica_groups=mesh['row_0'=8,'row_1'=2,'col_0'=4,'col_1'=8] {'row_0','row_1'}, dimensions={0}, use_global_device_ids=true | all-gather | bytes 557056 | tf_op jit(solution)/shard_map/all_gather | solution.py:65
  255.8 1.8 fusion
  257.6 1.2 convolution_bitcast_fusion
  258.8 0.2 copy.14
  259.0 20.8 %all_to_all.47 = f32[16,64,128]{2,1,0:T(8,128)S(1)} all-to-all(f32[16,64,128]{2,1,0:T(8,128)S(1)} %bitcast.91), channel_id=1, replica_groups=mesh['row_0'=8,'row_1'=2,'col_0'=4,'col_1'=8] {'row_0','row_1'}, dimensions={0} | all-to-all | bytes 1048576 | tf_op jit(solution)/shard_map/all_to_all | solution.py:43
  279.8 0.7 convolution_bitcast_fusion.2
  280.5 0.2 copy.15
  280.7 1.0 reshape.50
  281.7 4.7 %all-to-all-start.7 = ((f32[32,1,2048]{2,1,0:T(1,128)}), f32[32,1,2048]{2,1,0:T(1,128)S(1)}, u32[]{:S(2)}, u32[]{:S(2)}) async-start(f32[32,1,2048]{2,1,0:T(1,128)} %reshape.50), calls=%async_computation.7 | async-start | bytes 524288 | tf_op jit(solution)/shard_map/all_to_all | solution.py:43
  286.4 12.7 %all-to-all-done.7 = f32[32,1,2048]{2,1,0:T(1,128)S(1)} async-done(((f32[32,1,2048]{2,1,0:T(1,128)}), f32[32,1,2048]{2,1,0:T(1,128)S(1)}, u32[]{:S(2)}, u32[]{:S(2)}) %all-to-all-start.7) | async-done | bytes 262176 | tf_op jit(solution)/shard_map/all_to_all | solution.py:43
  299.1 1.3 reduce.3
  300.4 0.2 reshape.51
  300.6 0.1 reduce_sum.106
  300.6 0.7 multiply_reduce_fusion
  301.3 15.7 %all-reduce.2 = (f32[]{:T(128)}, f32[]{:T(128)}, f32[]{:T(128)}) all-reduce(f32[]{:T(128)} %get-tuple-element.3, f32[]{:T(128)} %get-tuple-element.4, f32[]{:T(128)} %get-tuple-element.2), channel_id=1, replica_groups=mesh['row_0'=8,'row_1'=2,'col_0'=4,'col_1'=8] {'row_0'}, use_global_device_ids=true, to_apply=%region_30.0 | all-reduce | flops 3 | bytes 24 | tf_op jit(solution)/shard_map/psum | solution.py:48
  317.0 3.1 all-reduce.6
  320.1 10.2 %all-reduce.4 = (f32[]{:T(128)}, f32[]{:T(128)}, f32[]{:T(128)}) all-reduce(f32[]{:T(128)} %get-tuple-element.26, f32[]{:T(128)} %get-tuple-element.27, f32[]{:T(128)} %get-tuple-element.28), channel_id=1, replica_groups=mesh['row_0'=8,'row_1'=2,'col_0'=4,'col_1'=8] {'col_0'}, use_global_device_ids=true, to_apply=%region_32.0 | all-reduce | flops 3 | bytes 24 | tf_op jit(solution)/shard_map/psum | solution.py:48
  330.3 17.3 %all-reduce = (f32[]{:T(128)}, f32[]{:T(128)}, f32[]{:T(128)}) all-reduce(f32[]{:T(128)} %get-tuple-element.20, f32[]{:T(128)} %get-tuple-element.21, f32[]{:T(128)} %get-tuple-element.22), channel_id=1, replica_groups=mesh['row_0'=8,'row_1'=2,'col_0'=4,'col_1'=8] {'col_1'}, use_global_device_ids=true, to_apply=%region_33.0 | all-reduce | flops 3 | bytes 24 | tf_op jit(solution)/shard_map/psum | solution.py:48
  350.6 0.7 subtract_divide_fusion
  351.3 0.6 pad_maximum_fusion
  (12 shorter events, 0.1 us)
Async XLA Ops:
  0.6 56.9 %copy-start = (f32[64,32]{0,1:T(8,128)S(1)}, f32[64,32]{0,1:T(8,128)}, u32[]{:S(2)}) copy-start(f32[64,32]{0,1:T(8,128)} %param.6) | copy-start | bytes 24580
  57.9 14.0 %copy-start.2 = (f32[128,64]{0,1:T(8,128)S(1)}, f32[128,64]{0,1:T(8,128)}, u32[]{:S(2)}) copy-start(f32[128,64]{0,1:T(8,128)} %param.10) | copy-start | bytes 98308
  72.0 20.4 %copy-start.3 = (f32[256,32]{0,1:T(8,128)S(1)}, f32[256,32]{0,1:T(8,128)}, u32[]{:S(2)}) copy-start(f32[256,32]{0,1:T(8,128)} %param.9) | copy-start | bytes 98308
  93.5 33.5 %all-to-all-start.2 = ((f32[32,256,32]{1,2,0:T(8,128)}), f32[32,256,32]{1,2,0:T(8,128)S(1)}, u32[]{:S(2)}, u32[]{:S(2)}) async-start(f32[32,256,32]{1,2,0:T(8,128)} %broadcast_in_dim.12), calls=%async_computation.2 | async-start | bytes 2097152 | tf_op jit(solution)/shard_map/all_to_all | solution.py:19
  101.2 25.9 %copy-start.1 = (f32[256,128]{1,0:T(8,128)S(1)}, f32[256,128]{1,0:T(8,128)}, u32[]{:S(2)}) copy-start(f32[256,128]{1,0:T(8,128)} %param.11) | copy-start | bytes 393220
  170.6 0.7 copy-start.4
  170.7 0.7 copy-start.5
  281.7 17.4 %all-to-all-start.7 = ((f32[32,1,2048]{2,1,0:T(1,128)}), f32[32,1,2048]{2,1,0:T(1,128)S(1)}, u32[]{:S(2)}, u32[]{:S(2)}) async-start(f32[32,1,2048]{2,1,0:T(1,128)} %reshape.50), calls=%async_computation.7 | async-start | bytes 524288 | tf_op jit(solution)/shard_map/all_to_all | solution.py:43
where the time goes:
time: 353 us; the launch traced here: 352 us
  blocking collectives  289 us (82%)
  waiting for transfers between devices  20.9 us (6%)
  matrix products  9.44 us (3%)
  other arithmetic  9.38 us (3%)
  starting transfers between devices  9.31 us (3%)
  between operations  7.88 us (2%)
  local copies, waits for them, and re-layouts  6.02 us (2%)
    psum x12, blocking collectives, over_axes(): return functools.reduce(lax.psum, axes, value)  147 us
    all_to_all x3, blocking collectives, sum_at_owner(): lax.all_to_all(parts, axis, split_axis=0, concat_axis=0, tiled=True)  58.4 us
    all_to_all x3, blocking collectives, copy_for_each(): lax.all_to_all(jnp.broadcast_to(value[None], (size, *value.shape)), axis,...  49.7 us
    all_gather x2, blocking collectives, shards(): image_columns = lax.all_gather(image_block, ROW, axis=0, tiled=True)  33.4 us
    all_to_all x1, waiting for transfers between devices, sum_at_owner(): lax.all_to_all(parts, axis, split_axis=0, concat_axis=0, tiled=True)  12.7 us
    all_to_all x1, waiting for transfers between devices, copy_for_each(): lax.all_to_all(jnp.broadcast_to(value[None], (size, *value.shape)), axis,...  8.16 us
  transfers between devices with their start and end apart: 2, of which 2 were waited for; matrix products, arithmetic and copies ran while one was open for 1% of the time, Pallas kernels for 0%

commit v1 on v0

--- a/solution.py
+++ b/solution.py
@@ -62,7 +62,9 @@
         panel_conduction = gathered_copies(psi_conduction, ROW, 1)
         full_rows = gathered_copies(vector, COL, 1)
         image_block = jnp.dot(full_rows, panel_conduction.T, precision=high)
-        image_columns = lax.all_gather(image_block, ROW, axis=0, tiled=True)
+        image_columns = jnp.concatenate(
+            lax.all_to_all(jnp.stack([image_block] * lax.axis_size(ROW)), ROW, 0, 0), axis=0
+        )
         points = jnp.dot(panel_valence, image_columns, precision=high)
         weighted = points * screened
         back_valence = sum_at_owner(jnp.dot(panel_valence.T, weighted, precision=high), ROW, 0)

time: 353 us -> 378 us (1.071)
  blocking collectives: 289 us -> 308 us
  waiting for transfers between devices: 20.9 us -> 25.1 us
    all_to_all x0 -> x2, blocking collectives: none -> 40.4 us  [shards(): lax.all_to_all(jnp.stack([image_block] * lax.axis_size(ROW)), ROW, 0, 0)]
    all_gather x2 -> x0, blocking collectives: 33.4 us -> none  [shards(): image_columns = lax.all_gather(image_block, ROW, axis=0, tiled=True)]
    all_to_all x3, blocking collectives: 49.7 us -> 62.8 us  [copy_for_each(): lax.all_to_all(jnp.broadcast_to(value[None], (size, *value.shape)), axis,...]
    all_to_all x1, waiting for transfers between devices: 8.16 us -> 12.4 us  [copy_for_each(): lax.all_to_all(jnp.broadcast_to(value[None], (size, *value.shape)), axis,...]
where the time goes in v1:
time: 378 us; the launch traced here: 377 us
  blocking collectives  308 us (81%)
  waiting for transfers between devices  25.1 us (7%)
  starting transfers between devices  10.9 us (3%)
  matrix products  9.43 us (2%)
  other arithmetic  9.38 us (2%)
  between operations  7.89 us (2%)
  local copies, waits for them, and re-layouts  5.9 us (2%)
    psum x12, blocking collectives, over_axes(): return functools.reduce(lax.psum, axes, value)  147 us
    all_to_all x3, blocking collectives, copy_for_each(): lax.all_to_all(jnp.broadcast_to(value[None], (size, *value.shape)), axis,...  62.8 us
    all_to_all x3, blocking collectives, sum_at_owner(): lax.all_to_all(parts, axis, split_axis=0, concat_axis=0, tiled=True)  57.7 us
    all_to_all x2, blocking collectives, shards(): lax.all_to_all(jnp.stack([image_block] * lax.axis_size(ROW)), ROW, 0, 0)  40.4 us
    all_to_all x1, waiting for transfers between devices, sum_at_owner(): lax.all_to_all(parts, axis, split_axis=0, concat_axis=0, tiled=True)  12.7 us
    all_to_all x1, waiting for transfers between devices, copy_for_each(): lax.all_to_all(jnp.broadcast_to(value[None], (size, *value.shape)), axis,...  12.4 us
  transfers between devices with their start and end apart: 2, of which 2 were waited for; matrix products, arithmetic and copies ran while one was open for 1% of the time, Pallas kernels for 0%

profile of v1, /device:TPU:8, one launch (start us, length us, event | category | flops | bytes accessed | tf_op | source)
XLA Modules:
  0.0 376.9 jit_solution(4137694335879759000)
XLA Ops:
  0.6 1.4 multiply_reduce_fusion.6
  2.0 20.6 %psum.196 = f32[]{:T(128)} all-reduce(f32[]{:T(128)} %multiply_reduce_fusion.6), channel_id=1, replica_groups=mesh['row_0'=8,'row_1'=2,'col_0'=4,'col_1'=8] {'row_0'}, use_global_device_ids=true, to_apply=%region_1.0 | all-reduce | flops 1 | bytes 8 | tf_op jit(solution)/shard_map/psum | solution.py:48
  22.6 3.1 psum.197
  25.7 8.3 %psum.198 = f32[]{:T(128)} all-reduce(f32[]{:T(128)} %psum.197), channel_id=1, replica_groups=mesh['row_0'=8,'row_1'=2,'col_0'=4,'col_1'=8] {'col_0'}, use_global_device_ids=true, to_apply=%region_3.0 | all-reduce | flops 1 | bytes 8 | tf_op jit(solution)/shard_map/psum | solution.py:48
  34.0 22.8 %psum.199 = f32[]{:T(128)} all-reduce(f32[]{:T(128)} %psum.198), channel_id=1, replica_groups=mesh['row_0'=8,'row_1'=2,'col_0'=4,'col_1'=8] {'col_1'}, use_global_device_ids=true, to_apply=%region_4.0 | all-reduce | flops 1 | bytes 8 | tf_op jit(solution)/shard_map/psum | solution.py:48
  57.5 0.1 broadcast_bitcast_fusion.1
  57.6 0.3 reshape.56
  57.9 0.0 copy-start.2
  57.9 14.0 %all_to_all.52 = f32[32,1,2048]{2,1,0:T(1,128)S(1)} all-to-all(f32[32,1,2048]{2,1,0:T(1,128)S(1)} %reshape.56), channel_id=1, replica_groups=mesh['row_0'=8,'row_1'=2,'col_0'=4,'col_1'=8] {'col_0','col_1'}, dimensions={0} | all-to-all | bytes 524288 | tf_op jit(solution)/shard_map/all_to_all | solution.py:19
  71.9 0.8 broadcast_in_dim.11
  72.8 6.2 %all-to-all-start.1 = ((f32[16,128,64]{1,2,0:T(8,128)}), f32[16,128,64]{1,2,0:T(8,128)S(1)}, u32[]{:S(2)}, u32[]{:S(2)}) async-start(f32[16,128,64]{1,2,0:T(8,128)} %broadcast_in_dim.11), calls=%async_computation.1 | async-start | bytes 1048576 | tf_op jit(solution)/shard_map/all_to_all | solution.py:19
  79.0 0.5 broadcast.10
  79.5 1.3 reduce
  80.8 0.2 reshape.57
  81.0 12.4 %all-to-all-done.1 = f32[16,128,64]{1,2,0:T(8,128)S(1)} async-done(((f32[16,128,64]{1,2,0:T(8,128)}), f32[16,128,64]{1,2,0:T(8,128)S(1)}, u32[]{:S(2)}, u32[]{:S(2)}) %all-to-all-start.1) | async-done | bytes 524320 | tf_op jit(solution)/shard_map/all_to_all | solution.py:19
  93.3 1.0 fusion.4
  94.4 20.0 %all_to_all.53 = f32[16,64,128]{2,1,0:T(8,128)S(1)} all-to-all(f32[16,64,128]{2,1,0:T(8,128)S(1)} %stack.14), channel_id=1, replica_groups=mesh['row_0'=8,'row_1'=2,'col_0'=4,'col_1'=8] {'row_0','row_1'}, dimensions={0} | all-to-all | bytes 1048576 | tf_op jit(solution)/shard_map/all_to_all | solution.py:66
  114.4 0.1 broadcast_in_dim.12
  114.6 33.5 %all_to_all.54 = f32[32,256,32]{1,2,0:T(8,128)S(1)} all-to-all(f32[32,256,32]{1,2,0:T(8,128)S(1)} %broadcast_in_dim.12), channel_id=1, replica_groups=mesh['row_0'=8,'row_1'=2,'col_0'=4,'col_1'=8] {'col_0','col_1'}, dimensions={0} | all-to-all | bytes 2097152 | tf_op jit(solution)/shard_map/all_to_all | solution.py:19
  148.0 1.8 fusion.1
  149.8 1.2 convolution_bitcast_fusion.1
  151.1 0.2 copy.12
  151.3 20.0 %all_to_all.55 = f32[16,64,128]{2,1,0:T(8,128)S(1)} all-to-all(f32[16,64,128]{2,1,0:T(8,128)S(1)} %bitcast.93), channel_id=1, replica_groups=mesh['row_0'=8,'row_1'=2,'col_0'=4,'col_1'=8] {'row_0','row_1'}, dimensions={0} | all-to-all | bytes 1048576 | tf_op jit(solution)/shard_map/all_to_all | solution.py:43
  171.4 0.7 convolution_bitcast_fusion.3
  172.0 0.2 copy.13
  172.2 0.3 reshape.58
  172.6 17.6 %all_to_all.56 = f32[32,1,2048]{2,1,0:T(1,128)S(1)} all-to-all(f32[32,1,2048]{2,1,0:T(1,128)S(1)} %reshape.58), channel_id=1, replica_groups=mesh['row_0'=8,'row_1'=2,'col_0'=4,'col_1'=8] {'col_0','col_1'}, dimensions={0} | all-to-all | bytes 524288 | tf_op jit(solution)/shard_map/all_to_all | solution.py:43
  190.2 1.3 reduce.1
  191.4 0.2 reshape.59
  191.7 0.1 reduce_sum.101
  191.8 0.6 copy-done.4
  192.3 0.0 copy-done.5
  192.3 0.7 multiply_reduce_fusion.3
  193.1 15.7 %all-reduce.3 = (f32[]{:T(128)}, f32[]{:T(128)}, f32[]{:T(128)}) all-reduce(f32[]{:T(128)} %get-tuple-element.6, f32[]{:T(128)} %get-tuple-element.7, f32[]{:T(128)} %get-tuple-element.5), channel_id=1, replica_groups=mesh['row_0'=8,'row_1'=2,'col_0'=4,'col_1'=8] {'row_0'}, use_global_device_ids=true, to_apply=%region_13.0 | all-reduce | flops 3 | bytes 24 | tf_op jit(solution)/shard_map/psum | solution.py:48
  208.8 3.1 all-reduce.7
  211.9 10.2 %all-reduce.5 = (f32[]{:T(128)}, f32[]{:T(128)}, f32[]{:T(128)}) all-reduce(f32[]{:T(128)} %get-tuple-element.29, f32[]{:T(128)} %get-tuple-element.30, f32[]{:T(128)} %get-tuple-element.31), channel_id=1, replica_groups=mesh['row_0'=8,'row_1'=2,'col_0'=4,'col_1'=8] {'col_0'}, use_global_device_ids=true, to_apply=%region_15.0 | all-reduce | flops 3 | bytes 24 | tf_op jit(solution)/shard_map/psum | solution.py:48
  222.2 17.3 %all-reduce.1 = (f32[]{:T(128)}, f32[]{:T(128)}, f32[]{:T(128)}) all-reduce(f32[]{:T(128)} %get-tuple-element.23, f32[]{:T(128)} %get-tuple-element.24, f32[]{:T(128)} %get-tuple-element.25), channel_id=1, replica_groups=mesh['row_0'=8,'row_1'=2,'col_0'=4,'col_1'=8] {'col_1'}, use_global_device_ids=true, to_apply=%region_16.0 | all-reduce | flops 3 | bytes 24 | tf_op jit(solution)/shard_map/psum | solution.py:48
  242.7 0.1 subtract_divide_fusion.1
  242.8 0.1 broadcast_bitcast_fusion
  242.8 0.3 reshape.60
  243.2 15.4 %all_to_all.57 = f32[32,1,2048]{2,1,0:T(1,128)S(1)} all-to-all(f32[32,1,2048]{2,1,0:T(1,128)S(1)} %reshape.60), channel_id=1, replica_groups=mesh['row_0'=8,'row_1'=2,'col_0'=4,'col_1'=8] {'col_0','col_1'}, dimensions={0} | all-to-all | bytes 524288 | tf_op jit(solution)/shard_map/all_to_all | solution.py:19
  258.5 1.3 reduce.2
  259.8 0.2 reshape.61
  260.0 1.0 fusion.5
  261.1 20.4 %all_to_all.58 = f32[16,64,128]{2,1,0:T(8,128)S(1)} all-to-all(f32[16,64,128]{2,1,0:T(8,128)S(1)} %stack.15), channel_id=1, replica_groups=mesh['row_0'=8,'row_1'=2,'col_0'=4,'col_1'=8] {'row_0','row_1'}, dimensions={0} | all-to-all | bytes 1048576 | tf_op jit(solution)/shard_map/all_to_all | solution.py:66
  281.5 1.8 fusion
  283.3 1.2 convolution_bitcast_fusion
  284.6 0.2 copy.14
  284.8 20.0 %all_to_all.59 = f32[16,64,128]{2,1,0:T(8,128)S(1)} all-to-all(f32[16,64,128]{2,1,0:T(8,128)S(1)} %bitcast.95), channel_id=1, replica_groups=mesh['row_0'=8,'row_1'=2,'col_0'=4,'col_1'=8] {'row_0','row_1'}, dimensions={0} | all-to-all | bytes 1048576 | tf_op jit(solution)/shard_map/all_to_all | solution.py:43
  304.8 0.7 convolution_bitcast_fusion.2
  305.5 0.2 copy.15
  305.7 1.0 reshape.62
  306.7 4.7 %all-to-all-start.9 = ((f32[32,1,2048]{2,1,0:T(1,128)}), f32[32,1,2048]{2,1,0:T(1,128)S(1)}, u32[]{:S(2)}, u32[]{:S(2)}) async-start(f32[32,1,2048]{2,1,0:T(1,128)} %reshape.62), calls=%async_computation.9 | async-start | bytes 524288 | tf_op jit(solution)/shard_map/all_to_all | solution.py:43
  311.4 12.7 %all-to-all-done.9 = f32[32,1,2048]{2,1,0:T(1,128)S(1)} async-done(((f32[32,1,2048]{2,1,0:T(1,128)}), f32[32,1,2048]{2,1,0:T(1,128)S(1)}, u32[]{:S(2)}, u32[]{:S(2)}) %all-to-all-start.9) | async-done | bytes 262176 | tf_op jit(solution)/shard_map/all_to_all | solution.py:43
  324.1 1.3 reduce.3
  325.3 0.2 reshape.63
  325.6 0.1 reduce_sum.106
  325.6 0.7 multiply_reduce_fusion
  326.3 15.7 %all-reduce.2 = (f32[]{:T(128)}, f32[]{:T(128)}, f32[]{:T(128)}) all-reduce(f32[]{:T(128)} %get-tuple-element.3, f32[]{:T(128)} %get-tuple-element.4, f32[]{:T(128)} %get-tuple-element.2), channel_id=1, replica_groups=mesh['row_0'=8,'row_1'=2,'col_0'=4,'col_1'=8] {'row_0'}, use_global_device_ids=true, to_apply=%region_30.0 | all-reduce | flops 3 | bytes 24 | tf_op jit(solution)/shard_map/psum | solution.py:48
  342.0 3.1 all-reduce.6
  345.1 10.2 %all-reduce.4 = (f32[]{:T(128)}, f32[]{:T(128)}, f32[]{:T(128)}) all-reduce(f32[]{:T(128)} %get-tuple-element.26, f32[]{:T(128)} %get-tuple-element.27, f32[]{:T(128)} %get-tuple-element.28), channel_id=1, replica_groups=mesh['row_0'=8,'row_1'=2,'col_0'=4,'col_1'=8] {'col_0'}, use_global_device_ids=true, to_apply=%region_32.0 | all-reduce | flops 3 | bytes 24 | tf_op jit(solution)/shard_map/psum | solution.py:48
  355.3 17.3 %all-reduce = (f32[]{:T(128)}, f32[]{:T(128)}, f32[]{:T(128)}) all-reduce(f32[]{:T(128)} %get-tuple-element.20, f32[]{:T(128)} %get-tuple-element.21, f32[]{:T(128)} %get-tuple-element.22), channel_id=1, replica_groups=mesh['row_0'=8,'row_1'=2,'col_0'=4,'col_1'=8] {'col_1'}, use_global_device_ids=true, to_apply=%region_33.0 | all-reduce | flops 3 | bytes 24 | tf_op jit(solution)/shard_map/psum | solution.py:48
  375.6 0.7 subtract_divide_fusion
  376.3 0.6 pad_maximum_fusion
  (14 shorter events, 0.2 us)
Async XLA Ops:
  0.6 56.9 %copy-start = (f32[64,32]{0,1:T(8,128)S(1)}, f32[64,32]{0,1:T(8,128)}, u32[]{:S(2)}) copy-start(f32[64,32]{0,1:T(8,128)} %param.6) | copy-start | bytes 24580
  57.9 14.0 %copy-start.2 = (f32[128,64]{0,1:T(8,128)S(1)}, f32[128,64]{0,1:T(8,128)}, u32[]{:S(2)}) copy-start(f32[128,64]{0,1:T(8,128)} %param.10) | copy-start | bytes 98308
  72.8 20.6 %all-to-all-start.1 = ((f32[16,128,64]{1,2,0:T(8,128)}), f32[16,128,64]{1,2,0:T(8,128)S(1)}, u32[]{:S(2)}, u32[]{:S(2)}) async-start(f32[16,128,64]{1,2,0:T(8,128)} %broadcast_in_dim.11), calls=%async_computation.1 | async-start | bytes 1048576 | tf_op jit(solution)/shard_map/all_to_all | solution.py:19
  94.4 20.0 %copy-start.3 = (f32[256,32]{0,1:T(8,128)S(1)}, f32[256,32]{0,1:T(8,128)}, u32[]{:S(2)}) copy-start(f32[256,32]{0,1:T(8,128)} %param.9) | copy-start | bytes 98308
  114.6 33.5 %copy-start.1 = (f32[256,128]{1,0:T(8,128)S(1)}, f32[256,128]{1,0:T(8,128)}, u32[]{:S(2)}) copy-start(f32[256,128]{1,0:T(8,128)} %param.11) | copy-start | bytes 393220
  191.7 0.7 copy-start.4
  191.7 0.7 copy-start.5
  306.7 17.4 %all-to-all-start.9 = ((f32[32,1,2048]{2,1,0:T(1,128)}), f32[32,1,2048]{2,1,0:T(1,128)S(1)}, u32[]{:S(2)}, u32[]{:S(2)}) async-start(f32[32,1,2048]{2,1,0:T(1,128)} %reshape.62), calls=%async_computation.9 | async-start | bytes 524288 | tf_op jit(solution)/shard_map/all_to_all | solution.py:43
